TPU v7x, 256 devices: a whole 4x4x8 slice. The times are simulated.
256 devices in a mesh: row: 8 (over z), col: 32 (over y, x, core).
Axes of the slice: x: 4, y: 4, z: 8, core: 2. Of those that a mesh axis runs over, the one named last changes fastest.
Arguments:
- amps: bfloat16 [384, 131072], P('row', 'col'), may hold values from -6 to 6
- integrals: bfloat16 [131072, 8192], P('col', 'row'), may hold values from -0.046875 to 0.046875
- cd_first: int32 [131072], P('col'), may hold values from 0 to 2399
- cd_second: int32 [131072], P('col'), may hold values from 0 to 2399
- ab_first: int32 [8192], P('row'), may hold values from 0 to 2399
- ab_second: int32 [8192], P('row'), may hold values from 0 to 2399
- occ_first: int32 [384], P('col'), may hold values from 0 to 199
- occ_second: int32 [384], P('col'), may hold values from 0 to 199
- virt_irrep: int32 [2400], replicated, may hold values from 0 to 7
- occ_energy: float32 [200], replicated, may hold values from -2 to -0.5
- virt_energy: float32 [2400], replicated, may hold values from 0.2 to 3
Outputs:
- update: float32 [384, 8192], P('col', 'row')
All inputs are finite; a program needn't handle non-finite values.
Results may differ from a plain program's by a relative error of at most 0.0003.
Values may be sent and summed in bfloat16 or wider, within the bound.
No kernel may reach another device: no remote copies, remote signals or barrier semaphores. Data moves between devices by JAX's collectives and lax.ppermute only.
A program may use at most 64 MiB of HBM per device.

v0:
```python
import jax
import jax.numpy as jnp
from jax import lax
from jax.sharding import PartitionSpec as P


def table_lookup(values_table, positions):
    row_width = 64
    row_count = -(-values_table.shape[0] // row_width)
    padded_table = jnp.pad(
        values_table, (0, row_count * row_width - values_table.shape[0])
    ).reshape(row_count, row_width)
    high_hot = (
        (positions // row_width)[:, None] == jnp.arange(row_count, dtype=jnp.int32)[None, :]
    ).astype(jnp.float32)
    low_hot = (
        (positions % row_width)[:, None] == jnp.arange(row_width, dtype=jnp.int32)[None, :]
    ).astype(jnp.float32)
    picked = jnp.dot(
        high_hot, padded_table, precision=lax.Precision.HIGHEST, preferred_element_type=jnp.float32
    )
    return jnp.sum(picked * low_hot, axis=1)


def irrep_of(labels_float, first_orb, second_orb):
    first_label = table_lookup(labels_float, first_orb).astype(jnp.int32)
    second_label = table_lookup(labels_float, second_orb).astype(jnp.int32)
    return jnp.bitwise_xor(first_label, second_label)


def on_device(
    amps,
    integrals,
    cd_first,
    cd_second,
    ab_first,
    ab_second,
    occ_first,
    occ_second,
    virt_irrep,
    occ_energy,
    virt_energy,
):
    labels_float = virt_irrep.astype(jnp.float32)
    irrep_cd = irrep_of(labels_float, cd_first, cd_second)
    irrep_ab = irrep_of(labels_float, ab_first, ab_second)
    masked = jnp.where(irrep_cd[:, None] == irrep_ab[None, :], integrals, jnp.zeros_like(integrals))
    partial_sums = jnp.dot(
        lax.all_gather(amps, "row", axis=0, tiled=True), masked, preferred_element_type=jnp.float32
    )
    own_rows = occ_first.shape[0]
    summed = lax.psum(partial_sums, "col")
    ladder = lax.dynamic_slice_in_dim(summed, lax.axis_index("col") * own_rows, own_rows, 0)
    virt_part = table_lookup(virt_energy, ab_first) + table_lookup(virt_energy, ab_second)
    occ_part = table_lookup(occ_energy, occ_first) + table_lookup(occ_energy, occ_second)
    denom = virt_part[None, :] - occ_part[:, None]
    return ladder / denom


def solution(mesh):
    in_specs = (
        P("row", "col"),
        P("col", "row"),
        P("col"),
        P("col"),
        P("row"),
        P("row"),
        P("col"),
        P("col"),
        P(),
        P(),
        P(),
    )
    out_specs = P("col", "row")
    return jax.shard_map(
        on_device, mesh=mesh, in_specs=in_specs, out_specs=out_specs, check_vma=False
    )
```

profile of v0, /device:TPU:6, one launch (start us, length us, event | category | flops | bytes accessed | tf_op | source)
XLA Modules:
  0.0 190.4 jit_solution(7204045527473177920)
XLA Ops:
  6.5 0.0 all-gather.2.cloned.1.call-start
  6.5 0.7 all-gather.2.cloned.1.call-update
  7.3 0.0 all-reduce.5.cloned.1.call-start
  7.3 0.7 convert_element_type.57
  8.0 0.1 reshape.50
  8.1 0.7 add_select_fusion.5
  8.8 0.6 fusion.8
  9.4 0.7 add_select_fusion.7
  10.1 0.6 fusion.7
  10.7 0.7 add_select_fusion.2
  11.4 0.7 fusion.5
  12.1 0.7 add_select_fusion
  12.8 0.7 fusion.6
  13.5 0.0 copy-start.2
  13.6 0.0 copy-start.1
  13.6 0.0 copy-start
  13.6 0.0 copy-start.3
  13.6 43.5 %all-gather.2.cloned.1.call-done = bf16[384,4096]{1,0:T(8,128)(2,1)} async-done(((bf16[48,4096]{1,0:T(8,128)(2,1)}), bf16[384,4096]{1,0:T(8,128)(2,1)}) %all-gather.2.cloned.1.call-update) | async-done | bytes 3145744 | tf_op jit(solution)/shard_map/all_gather | solution.py:49
  57.1 9.0 %fusion.4 = f32[384,1024]{1,0:T(8,128)} fusion(bf16[384,4096]{1,0:T(8,128)(2,1)} %all-gather.2.cloned.1.call-done, bf16[4096,1024]{1,0:T(8,128)(2,1)} %param.12, s32[1024]{0:T(1024)S(1)} %convert_xor_fusion.1, s32[4096]{0:T(1024)S(1)} %convert_xor_fusion), kind=kOutput, calls=%fused_computation.7 | convolution fusion | flops 3229614080 | bytes 13127680 | tf_op jit(solution)/shard_map/dot_general | solution.py:48
  66.1 0.0 all-reduce.5.cloned.1.call-update
  66.1 0.0 copy-done.2
  66.1 0.0 copy-done.1
  66.2 0.1 reshape.52
  66.2 0.0 copy-done
  66.2 0.1 reshape.51
  66.3 0.3 fusion.11
  66.6 0.0 copy-done.3
  66.6 0.3 fusion.12
  67.0 0.6 fusion.10
  67.5 0.6 fusion.9
  68.1 113.8 %all-reduce.5.cloned.1.call-done = f32[384,1024]{1,0:T(8,128)} async-done(((f32[384,1024]{1,0:T(8,128)}), f32[384,1024]{1,0:T(8,128)}) %all-reduce.5.cloned.1.call-update) | async-done | bytes 1572880 | tf_op jit(solution)/shard_map/psum | solution.py:52
  181.9 1.6 subtract_divide_fusion
  (9 shorter events, 0.1 us)
Async XLA Ops:
  6.5 50.5 %all-gather.2.cloned.1.call-start = ((), (), s32[]{:S(2)}) async-start(), calls=%async_computation | async-start | bytes 3538944 | tf_op jit(solution)/shard_map/all_gather | solution.py:49
  7.3 174.7 %all-reduce.5.cloned.1.call-start = ((), (), s32[]{:S(2)}) async-start(), calls=%async_computation.1 | async-start | bytes 3145728 | tf_op jit(solution)/shard_map/psum | solution.py:52
  13.5 52.5 %copy-start.2 = (s32[12]{0:T(128)S(1)}, s32[12]{0:T(128)}, u32[]{:S(2)}) copy-start(s32[12]{0:T(128)} %param.17) | copy-start | bytes 148
  13.6 52.6 %copy-start.1 = (f32[200]{0:T(256)S(1)}, f32[200]{0:T(256)}, u32[]{:S(2)}) copy-start(f32[200]{0:T(256)} %param.20) | copy-start | bytes 2404
  13.6 52.7 %copy-start = (f32[2400]{0:T(1024)S(1)}, f32[2400]{0:T(1024)}, u32[]{:S(2)}) copy-start(f32[2400]{0:T(1024)} %param.21) | copy-start | bytes 28804
  13.6 53.0 %copy-start.3 = (s32[12]{0:T(128)S(1)}, s32[12]{0:T(128)}, u32[]{:S(2)}) copy-start(s32[12]{0:T(128)} %param.18) | copy-start | bytes 148
Sparse Core Ops, SparseCore 0:
  9.1 47.8 all-gather.1
  66.2 115.6 all-reduce.4
where the time goes:
time: 191 us; the launch traced here: 190 us
  waiting for transfers between devices  158 us (83%)
  between operations  13.5 us (7%)
  matrix products  13.3 us (7%)
  other arithmetic  5.24 us (3%)
    psum x1, waiting for transfers between devices, on_device(): summed = lax.psum(partial_sums, 'col')  114 us
    all_gather x1, waiting for transfers between devices, on_device(): lax.all_gather(amps, 'row', axis=0, tiled=True)  43.5 us
    dot_general x1, matrix products, on_device(): jnp.dot(lax.all_gather(amps, 'row', axis=0, tiled=True), masked, preferre...  9 us
    dot_general x8, matrix products, table_lookup(): jnp.dot(high_hot, padded_table, precision=lax.Precision.HIGHEST, preferre...  4.28 us
  transfers between devices with their start and end apart: 2, of which 2 were waited for; matrix products, arithmetic and copies ran while one was open for 4% of the time, Pallas kernels for 0%

commit v1 on v0

--- a/solution.py
+++ b/solution.py
@@ -46,7 +46,11 @@
     irrep_ab = irrep_of(labels_float, ab_first, ab_second)
     masked = jnp.where(irrep_cd[:, None] == irrep_ab[None, :], integrals, jnp.zeros_like(integrals))
     partial_sums = jnp.dot(
-        lax.all_gather(amps, "row", axis=0, tiled=True), masked, preferred_element_type=jnp.float32
+        jnp.concatenate(
+            lax.all_to_all(jnp.stack([amps] * lax.axis_size("row")), "row", 0, 0), axis=0
+        ),
+        masked,
+        preferred_element_type=jnp.float32,
     )
     own_rows = occ_first.shape[0]
     summed = lax.psum(partial_sums, "col")

time: 191 us -> 222 us (1.16)
  waiting for transfers between devices: 158 us -> 182 us
  starting transfers between devices: 0.04 us -> 8.63 us
  other arithmetic: 5.24 us -> 1.72 us
  local copies, waits for them, and re-layouts: 0.27 us -> 3.33 us
    all_to_all x0 -> x1, waiting for transfers between devices: none -> 71 us  [on_device(): lax.all_to_all(jnp.stack([amps] * lax.axis_size('row')), 'row', 0, 0)]
    all_gather x1 -> x0, waiting for transfers between devices: 43.5 us -> none  [on_device(): lax.all_gather(amps, 'row', axis=0, tiled=True)]
    all_to_all x0 -> x1, starting transfers between devices: none -> 8.6 us  [on_device(): lax.all_to_all(jnp.stack([amps] * lax.axis_size('row')), 'row', 0, 0)]
    another operation x0 -> x1, local copies, waits for them, and re-layouts: none -> 3.06 us  [on_device(): jnp.stack([amps] * lax.axis_size('row'))]
    psum x1, waiting for transfers between devices: 114 us -> 111 us  [on_device(): summed = lax.psum(partial_sums, 'col')]
  transfers between devices with their start and end apart: 2 -> 2, of which waited for: 2 -> 2; matrix products, arithmetic and copies ran while one was open for 4% -> 2% of each run, Pallas kernels for 0% -> 0%
where the time goes in v1:
time: 222 us
  waiting for transfers between devices  182 us (82%)
  between operations  13.6 us (6%)
  matrix products  12.4 us (6%)
  starting transfers between devices  8.63 us (4%)
  local copies, waits for them, and re-layouts  3.33 us (2%)
    psum x1, waiting for transfers between devices, on_device(): summed = lax.psum(partial_sums, 'col')  111 us
    all_to_all x1, waiting for transfers between devices, on_device(): lax.all_to_all(jnp.stack([amps] * lax.axis_size('row')), 'row', 0, 0)  71 us
    all_to_all x1, starting transfers between devices, on_device(): lax.all_to_all(jnp.stack([amps] * lax.axis_size('row')), 'row', 0, 0)  8.6 us
    dot_general x1, matrix products, on_device(): jnp.dot(jnp.concatenate(lax.all_to_all(jnp.stack([amps] * lax.axis_size('...  8.1 us
  transfers between devices with their start and end apart: 2, of which 2 were waited for; matrix products, arithmetic and copies ran while one was open for 2% of the time, Pallas kernels for 0%

profile of v1, /device:TPU:6, one launch (start us, length us, event | category | flops | bytes accessed | tf_op | source)
XLA Modules:
  0.0 222.1 jit_solution(7581456613052457535)
XLA Ops:
  6.5 0.0 copy-start.2
  6.5 0.0 copy-start.4
  6.5 3.1 %stack.2 = bf16[8,48,4096]{2,1,0:T(8,128)(2,1)} broadcast(bf16[48,4096]{1,0:T(8,128)(2,1)} %param.11), dimensions={1,2} | broadcast | bytes 3538944 | tf_op jit(solution)/shard_map/stack | solution.py:50
  9.6 0.0 copy-start.5
  9.6 0.0 copy-start
  9.6 0.0 copy-start.1
  9.6 8.6 %all-to-all-start = ((bf16[8,48,4096]{2,1,0:T(8,128)(2,1)}), bf16[8,48,4096]{2,1,0:T(8,128)(2,1)S(1)}, u32[]{:S(2)}, u32[]{:S(2)}) async-start(bf16[8,48,4096]{2,1,0:T(8,128)(2,1)} %stack.2), calls=%async_computation | async-start | bytes 6291456 | tf_op jit(solution)/shard_map/all_to_all | solution.py:50
  18.2 0.0 all-reduce.5.cloned.1.call-start
  18.2 0.0 copy-done.2
  18.3 0.1 reshape.55
  18.4 0.0 copy-done.4
  18.4 0.6 fusion.8
  18.9 0.0 copy-done.5
  19.0 0.6 fusion.7
  19.6 0.0 copy-done
  19.6 0.7 fusion.6
  20.3 0.0 copy-done.1
  20.3 0.7 fusion.5
  21.0 71.0 %all-to-all-done = bf16[8,48,4096]{2,1,0:T(8,128)(2,1)S(1)} async-done(((bf16[8,48,4096]{2,1,0:T(8,128)(2,1)}), bf16[8,48,4096]{2,1,0:T(8,128)(2,1)S(1)}, u32[]{:S(2)}, u32[]{:S(2)}) %all-to-all-start) | async-done | bytes 3145760 | tf_op jit(solution)/shard_map/all_to_all | solution.py:50
  92.0 0.0 copy-start.7
  92.0 0.0 copy-start.6
  92.0 0.0 copy-start.3
  92.0 0.0 copy-start.8
  92.0 8.1 %fusion.4 = f32[384,1024]{1,0:T(8,128)} fusion(bf16[384,4096]{1,0:T(8,128)(2,1)S(1)} %bitcast.12, bf16[4096,1024]{1,0:T(8,128)(2,1)} %param.12, s32[1024]{0:T(1024)S(1)} %convert_xor_fusion.1, s32[4096]{0:T(1024)S(1)} %convert_xor_fusion), kind=kOutput, calls=%fused_computation.7 | convolution fusion | flops 3229614080 | bytes 13127680 | tf_op jit(solution)/shard_map/dot_general | solution.py:48
  100.1 0.0 all-reduce.5.cloned.1.call-update
  100.1 0.0 copy-done.7
  100.2 0.0 copy-done.6
  100.2 0.1 reshape.58
  100.3 0.0 copy-done.3
  100.3 0.1 reshape.57
  100.3 0.3 fusion.11
  100.6 0.0 copy-done.8
  100.7 0.3 fusion.12
  101.0 0.6 fusion.9
  101.6 0.6 fusion.10
  102.2 111.5 %all-reduce.5.cloned.1.call-done = f32[384,1024]{1,0:T(8,128)} async-done(((f32[384,1024]{1,0:T(8,128)}), f32[384,1024]{1,0:T(8,128)}) %all-reduce.5.cloned.1.call-update) | async-done | bytes 1572880 | tf_op jit(solution)/shard_map/psum | solution.py:56
  213.6 1.6 subtract_divide_fusion
  (14 shorter events, 0.1 us)
Async XLA Ops:
  6.5 11.7 %copy-start.2 = (s32[2400]{0:T(1024)S(1)}, s32[2400]{0:T(1024)}, u32[]{:S(2)}) copy-start(s32[2400]{0:T(1024)} %param.19) | copy-start | bytes 28804
  6.5 11.8 %copy-start.4 = (s32[1024]{0:T(1024)S(1)}, s32[1024]{0:T(1024)}, u32[]{:S(2)}) copy-start(s32[1024]{0:T(1024)} %param.16) | copy-start | bytes 12292
  9.6 9.4 %copy-start.5 = (s32[1024]{0:T(1024)S(1)}, s32[1024]{0:T(1024)}, u32[]{:S(2)}) copy-start(s32[1024]{0:T(1024)} %param.15) | copy-start | bytes 12292
  9.6 10.0 %copy-start = (s32[4096]{0:T(1024)S(1)}, s32[4096]{0:T(1024)}, u32[]{:S(2)}) copy-start(s32[4096]{0:T(1024)} %param.14) | copy-start | bytes 49156
  9.6 10.7 %copy-start.1 = (s32[4096]{0:T(1024)S(1)}, s32[4096]{0:T(1024)}, u32[]{:S(2)}) copy-start(s32[4096]{0:T(1024)} %param.13) | copy-start | bytes 49156
  9.6 82.4 %all-to-all-start = ((bf16[8,48,4096]{2,1,0:T(8,128)(2,1)}), bf16[8,48,4096]{2,1,0:T(8,128)(2,1)S(1)}, u32[]{:S(2)}, u32[]{:S(2)}) async-start(bf16[8,48,4096]{2,1,0:T(8,128)(2,1)} %stack.2), calls=%async_computation | async-start | bytes 6291456 | tf_op jit(solution)/shard_map/all_to_all | solution.py:50
  18.2 195.4 %all-reduce.5.cloned.1.call-start = ((), (), s32[]{:S(2)}) async-start(), calls=%async_computation.1 | async-start | bytes 3145728 | tf_op jit(solution)/shard_map/psum | solution.py:56
  92.0 8.1 %copy-start.7 = (s32[12]{0:T(128)S(1)}, s32[12]{0:T(128)}, u32[]{:S(2)}) copy-start(s32[12]{0:T(128)} %param.17) | copy-start | bytes 148
  92.0 8.2 %copy-start.6 = (f32[200]{0:T(256)S(1)}, f32[200]{0:T(256)}, u32[]{:S(2)}) copy-start(f32[200]{0:T(256)} %param.20) | copy-start | bytes 2404
  92.0 8.3 %copy-start.3 = (f32[2400]{0:T(1024)S(1)}, f32[2400]{0:T(1024)}, u32[]{:S(2)}) copy-start(f32[2400]{0:T(1024)} %param.21) | copy-start | bytes 28804
  92.0 8.7 %copy-start.8 = (s32[12]{0:T(128)S(1)}, s32[12]{0:T(128)}, u32[]{:S(2)}) copy-start(s32[12]{0:T(128)} %param.18) | copy-start | bytes 148
Sparse Core Ops, SparseCore 0:
  100.2 113.3 all-reduce.4
